TPU v7x, 32 devices: a whole 2x2x4 slice. The times are simulated.
32 devices in a mesh: grid: 4 (over z), orb: 4 (over y, core), pts: 2 (over x).
Axes of the slice: x: 2, y: 2, z: 4, core: 2. Of those that a mesh axis runs over, the one named last changes fastest.
Arguments:
- orbitals: bfloat16 [1024, 2048], P('grid', 'orb'), may hold values from -6 to 6
- points: int32 [8192], replicated, may hold values from 0 to 1023
- fitting: bfloat16 [1024, 8192], P('grid', ('orb', 'pts')), may hold values from -0.0625 to 0.0625
- screened: bfloat16 [8192, 8192], P(('orb', 'pts'), 'grid'), may hold values from -0.0014648438 to 0.0014648438
Outputs:
- exchange_orbitals: float32 [2048, 1024], P(('orb', 'pts'), 'grid')
- exchange_matrix: float32 [2048, 2048], P(('orb', 'pts'), 'grid')
Inputs may be any that keep to these rules, and one draw needn't show every extreme that they name: Grid rows of the window; two points may name the same row.
All inputs are finite; a program needn't handle non-finite values.
Results may differ from a plain program's by a relative error of at most 0.005.
Values may be sent and summed in bfloat16 or wider, within the bound.
A program may use at most 128 MiB of HBM per device.

v0:
```python
import math
import jax
import jax.numpy as jnp
from jax import lax
from jax.sharding import PartitionSpec as P


def per_device(orbitals, points, fitting, screened):
    grid_index = lax.axis_index("grid")
    orb_index = lax.axis_index("orb")
    pts_index = lax.axis_index("pts")
    n_grid = lax.axis_size("grid")
    n_orb = lax.axis_size("orb")
    n_pts = lax.axis_size("pts")
    rows_dev, width_dev = orbitals.shape
    npoints = points.shape[0]
    point_block = npoints // (n_orb * n_pts)
    column_block = npoints // n_grid
    local_rows = points - grid_index * rows_dev
    inside = (local_rows >= 0) & (local_rows < rows_dev)
    clamped = jnp.clip(local_rows, 0, rows_dev - 1)
    taken = jnp.take(orbitals, clamped, axis=0).astype(jnp.float32)
    selected = jnp.where(inside[:, None], taken, jnp.zeros_like(taken))
    picked = lax.psum(selected.astype(jnp.bfloat16), "grid")
    grouped = picked.reshape(n_orb, n_pts, point_block, width_dev)
    own_rows = lax.dynamic_index_in_dim(grouped, pts_index, 1, keepdims=False).reshape(
        n_orb * point_block, width_dev
    )
    point_rows = lax.dynamic_slice_in_dim(picked, grid_index * column_block, column_block, 0)
    rows_full, point_full = (
        lax.all_gather(own_rows, "orb", axis=1, tiled=True),
        lax.all_gather(point_rows, "orb", axis=1, tiled=True),
    )
    own_full = lax.dynamic_slice_in_dim(rows_full, orb_index * point_block, point_block, 0)
    density = lax.dot_general(
        own_full, point_full, (((1,), (1,)), ((), ())), preferred_element_type=jnp.float32
    )
    masked = (density * screened.astype(jnp.float32)).astype(jnp.bfloat16)
    partial_applied = jnp.dot(masked, point_full, preferred_element_type=jnp.float32)
    applied = lax.psum(partial_applied, "grid").astype(jnp.bfloat16)
    terms = lax.psum_scatter(
        -lax.dot_general(
            applied, fitting, (((0,), (1,)), ((), ())), preferred_element_type=jnp.float32
        ),
        ("orb", "pts"),
        scatter_dimension=0,
        tiled=True,
    )
    rounded = terms.astype(jnp.bfloat16)
    partial_matrix = jnp.dot(
        rounded,
        lax.all_gather(orbitals, "orb", axis=1, tiled=True),
        preferred_element_type=jnp.float32,
    )
    summed = lax.psum_scatter(partial_matrix, "grid", scatter_dimension=1, tiled=True)
    exchange_matrix = summed / math.sqrt(rows_dev * n_grid)
    return (terms, exchange_matrix)


def solution(mesh):
    in_specs = (P("grid", "orb"), P(), P("grid", ("orb", "pts")), P(("orb", "pts"), "grid"))
    out_specs = (P(("orb", "pts"), "grid"), P(("orb", "pts"), "grid"))
    return jax.shard_map(
        per_device, mesh=mesh, in_specs=in_specs, out_specs=out_specs, check_vma=False
    )
```

profile of v0, /device:TPU:0, one launch (start us, length us, event | category | flops | bytes accessed | tf_op | source)
XLA Modules:
  0.0 927.6 jit_solution(6591598182595387034)
XLA Ops:
  7.2 0.0 all-reduce.3.cloned.1.call-start
  7.2 0.8 compare_and_fusion.1
  8.1 0.8 fusion.11
  8.8 34.9 %gather_fusion = bf16[8192,512]{1,0:T(8,128)(2,1)} fusion(bf16[256,512]{1,0:T(8,128)(2,1)} %param.4, s32[8192]{0:T(1024)S(1)} %fusion.11), kind=kCustom, calls=%fused_computation | custom fusion | bytes 16809984 | tf_op jit(solution)/shard_map/jit(_take)/gather | solution.py:22
  43.8 8.5 select_convert_fusion
  52.3 0.0 all-gather.6.cloned.1.call-start
  52.4 293.7 %all-reduce.3.cloned.1.call-done = bf16[8192,512]{1,0:T(8,128)(2,1)} async-done(((bf16[8192,512]{1,0:T(8,128)(2,1)}), bf16[8192,512]{1,0:T(8,128)(2,1)}) %all-reduce.3.cloned.1.call-update) | async-done | bytes 8388624 | tf_op jit(solution)/shard_map/psum | solution.py:24
  346.0 3.0 constant_dynamic-slice_fusion
  349.1 0.0 all-gather.4.cloned.1.call-start
  349.2 4.4 constant_dynamic-slice_fusion.1
  353.6 0.0 all-gather.8.cloned.1.call-start
  353.7 0.5 all-gather.8.cloned.1.call-update
  354.2 0.0 reduce-scatter.3.cloned.1.call-start
  354.2 52.3 %all-gather.6.cloned.1.call-done = bf16[2048,2048]{1,0:T(8,128)(2,1)} async-done(((bf16[2048,512]{1,0:T(8,128)(2,1)}), bf16[2048,2048]{1,0:T(8,128)(2,1)}) %all-gather.6.cloned.1.call-update) | async-done | bytes 8388624 | tf_op jit(solution)/shard_map/all_gather | solution.py:32
  406.5 107.5 %all-gather.4.cloned.1.call-done = bf16[4096,2048]{1,0:T(8,128)(2,1)} async-done(((bf16[4096,512]{1,0:T(8,128)(2,1)}), bf16[4096,2048]{1,0:T(8,128)(2,1)}) %all-gather.4.cloned.1.call-update) | async-done | bytes 16777232 | tf_op jit(solution)/shard_map/all_gather | solution.py:31
  514.0 27.6 %fusion.4 = f32[1024,2048]{1,0:T(8,128)} fusion(bf16[2048,2048]{1,0:T(8,128)(2,1)} %all-gather.6.cloned.1.call-done, bf16[1024,2048]{1,0:T(8,128)(2,1)} %param.7, bf16[4096,2048]{1,0:T(8,128)(2,1)} %all-gather.4.cloned.1.call-done, s32[]{:T(128)S(6)} %select_n.27), kind=kOutput, calls=%fused_computation.6 | convolution fusion | flops 17186160640 | bytes 33554436 | tf_op jit(solution)/shard_map/dot_general | solution.py:39
  541.6 286.5 %all-reduce.4 = bf16[1024,2048]{1,0:T(8,128)(2,1)} all-reduce(f32[1024,2048]{1,0:T(8,128)} %fusion.4), channel_id=1, replica_groups=mesh['grid'=4,'orb'=4,'pts'=2] {'grid'}, use_global_device_ids=true, to_apply=%region_1.2 | all-reduce | flops 2097152 | bytes 12582912 | tf_op jit(solution)/shard_map/psum | solution.py:40
  828.1 4.8 fusion.6
  833.0 0.0 reduce-scatter.5.cloned.1.call-start
  833.0 0.0 all-gather.8.cloned.1.call-done
  833.1 38.9 %reduce-scatter.3.cloned.1.call-done = f32[256,256]{1,0:T(8,128)} async-done(((f32[2048,256]{1,0:T(8,128)}), f32[256,256]{1,0:T(8,128)}) %reduce-scatter.3.cloned.1.call-update) | async-done | bytes 262160 | tf_op jit(solution)/shard_map/reduce_scatter | solution.py:41
  872.0 3.1 fusion.9
  875.1 43.8 %reduce-scatter.5.cloned.1.call-done = f32[256,512]{1,0:T(8,128)} async-done(((f32[256,2048]{1,0:T(8,128)}), f32[256,512]{1,0:T(8,128)}) %reduce-scatter.5.cloned.1.call-update) | async-done | bytes 524304 | tf_op jit(solution)/shard_map/reduce_scatter | solution.py:55
  918.9 1.9 broadcast_multiply_fusion
  (7 shorter events, 0.1 us)
Async XLA Ops:
  7.2 821.0 %copy-start = (bf16[256,1024]{1,0:T(8,128)(2,1)S(1)}, bf16[256,1024]{1,0:T(8,128)(2,1)}, u32[]{:S(2)}) copy-start(bf16[256,1024]{1,0:T(8,128)(2,1)} %param.6) | copy-start | bytes 1572868
  7.2 338.9 %all-reduce.3.cloned.1.call-start = ((), (), s32[]{:S(2)}) async-start(), calls=%async_computation.2 | async-start | bytes 16777216 | tf_op jit(solution)/shard_map/psum | solution.py:24
  52.3 354.2 %all-gather.6.cloned.1.call-start = ((), (), s32[]{:S(2)}) async-start(), calls=%async_computation.4 | async-start | bytes 10485760 | tf_op jit(solution)/shard_map/all_gather | solution.py:32
  349.1 164.9 %all-gather.4.cloned.1.call-start = ((), (), s32[]{:S(2)}) async-start(), calls=%async_computation.3 | async-start | bytes 20971520 | tf_op jit(solution)/shard_map/all_gather | solution.py:31
  353.6 479.4 %all-gather.8.cloned.1.call-start = ((), (), s32[]{:S(2)}) async-start(), calls=%async_computation.6 | async-start | bytes 1310720 | tf_op jit(solution)/shard_map/all_gather | solution.py:52
  354.2 517.8 %reduce-scatter.3.cloned.1.call-start = ((), (), s32[]{:S(2)}) async-start(), calls=%async_computation.5 | async-start | bytes 2359296 | tf_op jit(solution)/shard_map/reduce_scatter | solution.py:41
  833.0 85.9 %reduce-scatter.5.cloned.1.call-start = ((), (), s32[]{:S(2)}) async-start(), calls=%async_computation.7 | async-start | bytes 2621440 | tf_op jit(solution)/shard_map/reduce_scatter | solution.py:55
Sparse Core Ops, SparseCore 0:
  52.5 293.5 all-reduce.2
  349.2 57.2 all-gather.5
  408.1 105.8 all-gather.3
  515.4 16.6 all-gather.7
  833.1 38.8 reduce-scatter.2
  875.2 43.5 reduce-scatter.4
where the time goes:
time: 928 us
  waiting for transfers between devices  537 us (58%)
  blocking collectives  287 us (31%)
  local copies, waits for them, and re-layouts  42.4 us (5%)
  matrix products  35.5 us (4%)
  between operations  14.2 us (2%)
  other arithmetic  12 us (1%)
    psum x1, waiting for transfers between devices, per_device(): picked = lax.psum(selected.astype(jnp.bfloat16), 'grid')  294 us
    psum x1, blocking collectives, per_device(): applied = lax.psum(partial_applied, 'grid').astype(jnp.bfloat16)  287 us
    all_gather x1, waiting for transfers between devices, per_device(): lax.all_gather(own_rows, 'orb', axis=1, tiled=True)  107 us
    all_gather x1, waiting for transfers between devices, per_device(): lax.all_gather(point_rows, 'orb', axis=1, tiled=True)  52.3 us
    reduce_scatter x1, waiting for transfers between devices, per_device(): lax.psum_scatter(partial_matrix, 'grid', scatter_dimension=1, tiled=True)  43.8 us
    reduce_scatter x1, waiting for transfers between devices, per_device(): lax.psum_scatter(-lax.dot_general(applied, fitting, (((0,), (1,)), ((), (...  38.9 us
    gather x1, local copies, waits for them, and re-layouts, per_device(): taken = jnp.take(orbitals, clamped, axis=0).astype(jnp.float32)  34.9 us
    dot_general x1, matrix products, per_device(): jnp.dot(masked, point_full, preferred_element_type=jnp.float32)  27.6 us
  transfers between devices with their start and end apart: 6, of which 5 were waited for; matrix products, arithmetic and copies ran while one was open for 4% of the time, Pallas kernels for 0%

commit v1 on v0

--- a/solution.py
+++ b/solution.py
@@ -21,7 +21,8 @@
     clamped = jnp.clip(local_rows, 0, rows_dev - 1)
     taken = jnp.take(orbitals, clamped, axis=0).astype(jnp.float32)
     selected = jnp.where(inside[:, None], taken, jnp.zeros_like(taken))
-    picked = lax.psum(selected.astype(jnp.bfloat16), "grid")
+    stops_all_set = lambda content: jnp.sum(lax.all_gather(content, "grid"), axis=0)
+    picked = stops_all_set(selected.astype(jnp.bfloat16))
     grouped = picked.reshape(n_orb, n_pts, point_block, width_dev)
     own_rows = lax.dynamic_index_in_dim(grouped, pts_index, 1, keepdims=False).reshape(
         n_orb * point_block, width_dev

time: 928 us -> 1220 us (1.31)
  waiting for transfers between devices: 537 us -> 807 us
  other arithmetic: 12 us -> 28.4 us
    all_gather x0 -> x1, waiting for transfers between devices: none -> 564 us  [per_device(): lax.all_gather(content, 'grid')]
    psum x1 -> x0, waiting for transfers between devices: 294 us -> none  [per_device(): picked = lax.psum(selected.astype(jnp.bfloat16), 'grid')]
    reduce_sum x0 -> x1, other arithmetic: none -> 16.3 us  [per_device(): jnp.sum(lax.all_gather(content, 'grid'), axis=0)]
  transfers between devices with their start and end apart: 6 -> 6, of which waited for: 5 -> 5; matrix products, arithmetic and copies ran while one was open for 4% -> 3% of each run, Pallas kernels for 0% -> 0%
where the time goes in v1:
time: 1220 us; the launch traced here: 1210 us
  waiting for transfers between devices  807 us (66%)
  blocking collectives  287 us (24%)
  local copies, waits for them, and re-layouts  42.4 us (3%)
  matrix products  35.6 us (3%)
  other arithmetic  28.4 us (2%)
  between operations  14.1 us (1%)
    all_gather x1, waiting for transfers between devices, per_device(): lax.all_gather(content, 'grid')  564 us
    psum x1, blocking collectives, per_device(): applied = lax.psum(partial_applied, 'grid').astype(jnp.bfloat16)  287 us
    all_gather x1, waiting for transfers between devices, per_device(): lax.all_gather(own_rows, 'orb', axis=1, tiled=True)  107 us
    all_gather x1, waiting for transfers between devices, per_device(): lax.all_gather(point_rows, 'orb', axis=1, tiled=True)  51.5 us
    reduce_scatter x1, waiting for transfers between devices, per_device(): lax.psum_scatter(partial_matrix, 'grid', scatter_dimension=1, tiled=True)  43.8 us
    reduce_scatter x1, waiting for transfers between devices, per_device(): lax.psum_scatter(-lax.dot_general(applied, fitting, (((0,), (1,)), ((), (...  39.1 us
    gather x1, local copies, waits for them, and re-layouts, per_device(): taken = jnp.take(orbitals, clamped, axis=0).astype(jnp.float32)  34.9 us
    dot_general x1, matrix products, per_device(): jnp.dot(masked, point_full, preferred_element_type=jnp.float32)  27.6 us
  transfers between devices with their start and end apart: 6, of which 5 were waited for; matrix products, arithmetic and copies ran while one was open for 3% of the time, Pallas kernels for 0%

profile of v1, /device:TPU:0, one launch (start us, length us, event | category | flops | bytes accessed | tf_op | source)
XLA Modules:
  0.0 1214.7 jit_solution(13406106823982599792)
XLA Ops:
  7.2 0.0 all-gather.5.cloned.1.call-start
  7.2 0.8 compare_and_fusion.1
  8.1 0.8 fusion.11
  8.8 34.9 %gather_fusion = bf16[8192,512]{1,0:T(8,128)(2,1)} fusion(bf16[256,512]{1,0:T(8,128)(2,1)} %param.4, s32[8192]{0:T(1024)S(1)} %fusion.11), kind=kCustom, calls=%fused_computation | custom fusion | bytes 16809984 | tf_op jit(solution)/shard_map/jit(_take)/gather | solution.py:22
  43.7 8.6 select_convert_fusion
  52.3 0.0 all-gather.9.cloned.1.call-start
  52.4 564.2 %all-gather.5.cloned.1.call-done = bf16[4,8192,512]{2,1,0:T(8,128)(2,1)} async-done(((bf16[1,8192,512]{2,1,0:T(8,128)(2,1)}), bf16[4,8192,512]{2,1,0:T(8,128)(2,1)}) %all-gather.5.cloned.1.call-update) | async-done | bytes 33554448 | tf_op jit(solution)/shard_map/all_gather | solution.py:24
  616.6 16.3 %reduce_sum.12 = bf16[8192,512]{1,0:T(8,128)(2,1)} reduce(bf16[4,8192,512]{2,1,0:T(8,128)(2,1)} %all-gather.5.cloned.1.call-done, bf16[]{:T(256)} %constant.21.clone.1), dimensions={0}, to_apply=%region_0.1 | reduce | flops 12582912 | bytes 41943040 | tf_op jit(solution)/shard_map/reduce_sum | solution.py:24
  632.9 3.0 constant_dynamic-slice_fusion
  636.0 0.0 all-gather.7.cloned.1.call-start
  636.0 4.4 constant_dynamic-slice_fusion.1
  640.5 0.0 all-gather.11.cloned.1.call-start
  640.5 0.5 all-gather.11.cloned.1.call-update
  641.0 0.0 reduce-scatter.3.cloned.1.call-start
  641.1 51.5 %all-gather.9.cloned.1.call-done = bf16[2048,2048]{1,0:T(8,128)(2,1)} async-done(((bf16[2048,512]{1,0:T(8,128)(2,1)}), bf16[2048,2048]{1,0:T(8,128)(2,1)}) %all-gather.9.cloned.1.call-update) | async-done | bytes 8388624 | tf_op jit(solution)/shard_map/all_gather | solution.py:33
  692.6 107.5 %all-gather.7.cloned.1.call-done = bf16[4096,2048]{1,0:T(8,128)(2,1)} async-done(((bf16[4096,512]{1,0:T(8,128)(2,1)}), bf16[4096,2048]{1,0:T(8,128)(2,1)}) %all-gather.7.cloned.1.call-update) | async-done | bytes 16777232 | tf_op jit(solution)/shard_map/all_gather | solution.py:32
  800.1 27.6 %fusion.4 = f32[1024,2048]{1,0:T(8,128)} fusion(bf16[2048,2048]{1,0:T(8,128)(2,1)} %all-gather.9.cloned.1.call-done, bf16[1024,2048]{1,0:T(8,128)(2,1)} %param.7, bf16[4096,2048]{1,0:T(8,128)(2,1)} %all-gather.7.cloned.1.call-done, s32[]{:T(128)S(6)} %select_n.41), kind=kOutput, calls=%fused_computation.7 | convolution fusion | flops 17186160640 | bytes 33554436 | tf_op jit(solution)/shard_map/dot_general | solution.py:40
  827.7 287.3 %all-reduce.1 = bf16[1024,2048]{1,0:T(8,128)(2,1)} all-reduce(f32[1024,2048]{1,0:T(8,128)} %fusion.4), channel_id=1, replica_groups=mesh['grid'=4,'orb'=4,'pts'=2] {'grid'}, use_global_device_ids=true, to_apply=%region_1.2 | all-reduce | flops 2097152 | bytes 12582912 | tf_op jit(solution)/shard_map/psum | solution.py:41
  1115.0 4.8 fusion.6
  1119.9 0.0 reduce-scatter.5.cloned.1.call-start
  1119.9 39.1 %reduce-scatter.3.cloned.1.call-done = f32[256,256]{1,0:T(8,128)} async-done(((f32[2048,256]{1,0:T(8,128)}), f32[256,256]{1,0:T(8,128)}) %reduce-scatter.3.cloned.1.call-update) | async-done | bytes 262160 | tf_op jit(solution)/shard_map/reduce_scatter | solution.py:42
  1159.1 3.1 fusion.9
  1162.2 43.8 %reduce-scatter.5.cloned.1.call-done = f32[256,512]{1,0:T(8,128)} async-done(((f32[256,2048]{1,0:T(8,128)}), f32[256,512]{1,0:T(8,128)}) %reduce-scatter.5.cloned.1.call-update) | async-done | bytes 524304 | tf_op jit(solution)/shard_map/reduce_scatter | solution.py:56
  1206.0 1.9 broadcast_multiply_fusion
  (8 shorter events, 0.1 us)
Async XLA Ops:
  7.2 1107.8 %copy-start = (bf16[256,1024]{1,0:T(8,128)(2,1)S(1)}, bf16[256,1024]{1,0:T(8,128)(2,1)}, u32[]{:S(2)}) copy-start(bf16[256,1024]{1,0:T(8,128)(2,1)} %param.6) | copy-start | bytes 1572868
  7.2 609.4 %all-gather.5.cloned.1.call-start = ((), (), s32[]{:S(2)}) async-start(), calls=%async_computation.2 | async-start | bytes 41943040 | tf_op jit(solution)/shard_map/all_gather | solution.py:24
  52.3 640.2 %all-gather.9.cloned.1.call-start = ((), (), s32[]{:S(2)}) async-start(), calls=%async_computation.4 | async-start | bytes 10485760 | tf_op jit(solution)/shard_map/all_gather | solution.py:33
  636.0 164.1 %all-gather.7.cloned.1.call-start = ((), (), s32[]{:S(2)}) async-start(), calls=%async_computation.3 | async-start | bytes 20971520 | tf_op jit(solution)/shard_map/all_gather | solution.py:32
  640.5 479.5 %all-gather.11.cloned.1.call-start = ((), (), s32[]{:S(2)}) async-start(), calls=%async_computation.6 | async-start | bytes 1310720 | tf_op jit(solution)/shard_map/all_gather | solution.py:53
  641.0 518.0 %reduce-scatter.3.cloned.1.call-start = ((), (), s32[]{:S(2)}) async-start(), calls=%async_computation.5 | async-start | bytes 2359296 | tf_op jit(solution)/shard_map/reduce_scatter | solution.py:42
  1119.9 86.1 %reduce-scatter.5.cloned.1.call-start = ((), (), s32[]{:S(2)}) async-start(), calls=%async_computation.7 | async-start | bytes 2621440 | tf_op jit(solution)/shard_map/reduce_scatter | solution.py:56
Sparse Core Ops, SparseCore 0:
  52.4 564.0 all-gather.4
  636.1 56.4 all-gather.8
  694.1 105.8 all-gather.6
  801.5 16.6 all-gather.10
  1120.0 39.0 reduce-scatter.2
  1162.3 43.6 reduce-scatter.4
